TPU v7x, 32 devices: a whole 2x2x4 slice. The times are simulated.
32 devices in a mesh: src: 8 (over y, x, core), tgt: 4 (over z).
Axes of the slice: x: 2, y: 2, z: 4, core: 2. Of those that a mesh axis runs over, the one named last changes fastest.
Arguments:
- src_emb: bfloat16 [64, 131072], P(None, 'src'), may hold values from -3 to 3
- tgt_emb: bfloat16 [64, 65536], P(None, 'tgt'), may hold values from -3 to 3
- src_hidden: bfloat16 [64, 131072], P(None, 'src'), may hold values from -4 to 4
- growth: float32 [131072], P('src'), may hold values from -1 to 1
- tgt_mass: float32 [65536], P('tgt'), may hold values from 0.5 to 2
- pair_code: int32 [8, 4, 512], P('src', 'tgt'), may hold values from 0 to 16383, as said below
- pair_count: int32 [8, 4], P('src', 'tgt'), may hold values from 128 to 512, as said below
- block_batch: int32 [1024], P('src'), may hold values from 0 to 31
Outputs:
- src_potential: float32 [131072], P('src')
- tgt_potential: float32 [65536], P('tgt')
- tgt_grad: float32 [64, 65536], P(None, 'tgt')
- adapter_grad: float32 [32, 64, 64], P(('src', 'tgt'))
Inputs may be any that keep to these rules, and one draw needn't show every extreme that they name: `pair_code`: the codes of one device are distinct; among the first 128 entries of each device's list every one of its 128 source blocks and every one of its 128 target blocks appears. `pair_count`: in every draw some device has all 512 entries live.
All inputs are finite; a program needn't handle non-finite values.
Results may differ from a plain program's by a relative error of at most 0.0003.
Values sent between devices are 32-bit elements; how exact they have to be, the bound alone decides.
A program may use at most 192 MiB of HBM per device.

v0:
```python
import math
import jax
import jax.numpy as jnp
from jax import lax
from jax.sharding import PartitionSpec as P

BLK = 128
ENC_DEV = 1
ITERS = 2
entropy_scale = 0.5
update_power = 0.4
highest = lax.Precision.HIGHEST


def rescale(scaling, masses, totals):
    return jnp.sqrt(scaling) * jnp.power(masses / totals, update_power)


def pick_blocks(selector, blocks):
    picked = jnp.einsum(
        "gb,dbi->dgi", selector.astype(jnp.bfloat16), blocks, preferred_element_type=jnp.float32
    )
    return picked.astype(jnp.bfloat16)


def per_device(src_emb, tgt_emb, src_hidden, growth, tgt_mass, pair_code, pair_count, block_batch):
    feat_width = src_emb.shape[0]
    src_blocks = src_emb.shape[1] // BLK
    tgt_blocks = tgt_emb.shape[1] // BLK
    src_cells = src_blocks * BLK
    tgt_cells = tgt_blocks * BLK
    slot_count = pair_code.shape[2]
    group_size = math.gcd(slot_count, 64)
    group_count = slot_count // group_size
    pair_slots = pair_code.reshape(slot_count)
    alive_mask = (jnp.arange(slot_count, dtype=jnp.int32) < pair_count.reshape(())).astype(
        jnp.float32
    )
    src_ids = pair_slots // tgt_blocks
    tgt_ids = pair_slots % tgt_blocks
    src_select = (src_ids[:, None] == jnp.arange(src_blocks, dtype=jnp.int32)[None, :]).astype(
        jnp.float32
    )
    tgt_select = (tgt_ids[:, None] == jnp.arange(tgt_blocks, dtype=jnp.int32)[None, :]).astype(
        jnp.float32
    )
    x_blocks = src_emb.reshape(feat_width, src_blocks, BLK)
    y_blocks = tgt_emb.reshape(feat_width, tgt_blocks, BLK)
    x_norms = jnp.sum(jnp.square(x_blocks.astype(jnp.float32)), axis=0)
    y_norms = jnp.sum(jnp.square(y_blocks.astype(jnp.float32)), axis=0)
    src_sel_groups = src_select.reshape(group_count, group_size, src_blocks)
    tgt_sel_groups = tgt_select.reshape(group_count, group_size, tgt_blocks)

    def kernel_group(inputs):
        src_sel, tgt_sel, alive_group = inputs
        x_part = pick_blocks(src_sel, x_blocks)
        y_part = pick_blocks(tgt_sel, y_blocks)
        inner_prods = jnp.einsum("dgi,dgj->gij", x_part, y_part, preferred_element_type=jnp.float32)
        x_sq = jnp.dot(src_sel, x_norms, precision=highest)
        y_sq = jnp.dot(tgt_sel, y_norms, precision=highest)
        distance = (x_sq[:, :, None] + y_sq[:, None, :] - 2.0 * inner_prods) / feat_width
        return jnp.exp(-distance / entropy_scale) * alive_group[:, None, None]

    kernel = lax.map(
        kernel_group, (src_sel_groups, tgt_sel_groups, alive_mask.reshape(group_count, group_size))
    )
    kernel = kernel.reshape(slot_count, BLK, BLK)
    src_mass = jnp.exp(growth)
    src_scale = jnp.ones((src_cells,), jnp.float32)
    tgt_scale = jnp.ones((tgt_cells,), jnp.float32)
    for iteration in range(ITERS):
        tgt_picked = jnp.dot(tgt_select, tgt_scale.reshape(tgt_blocks, BLK), precision=highest)
        src_picked = jnp.dot(src_select, src_scale.reshape(src_blocks, BLK), precision=highest)
        row_slots = jnp.einsum("pij,pj->pi", kernel, tgt_picked, precision=highest)
        col_slots = jnp.einsum("pij,pi->pj", kernel, src_picked, precision=highest)
        row_part = jnp.dot(src_select.T, row_slots, precision=highest).reshape(src_cells)
        col_part = jnp.dot(tgt_select.T, col_slots, precision=highest).reshape(tgt_cells)
        row_sums = lax.psum(row_part, "tgt")
        col_sums = lax.psum(col_part, "src")
        src_scale, tgt_scale = (
            rescale(src_scale, src_mass, row_sums),
            rescale(tgt_scale, tgt_mass, col_sums),
        )
    src_potential = entropy_scale * jnp.log(src_scale)
    tgt_potential = entropy_scale * jnp.log(tgt_scale)
    src_blocked = src_scale.reshape(src_blocks, BLK)
    tgt_blocked = tgt_scale.reshape(tgt_blocks, BLK)

    def gradient_group(carry, inputs):
        dx_total, dy_total = carry
        src_sel, tgt_sel, kernel_part = inputs
        row_scale = jnp.dot(src_sel, src_blocked, precision=highest)
        col_scale = jnp.dot(tgt_sel, tgt_blocked, precision=highest)
        transport = row_scale[:, :, None] * kernel_part * col_scale[:, None, :]
        plan_bf16 = transport.astype(jnp.bfloat16)
        x_part = pick_blocks(src_sel, x_blocks)
        y_part = pick_blocks(tgt_sel, y_blocks)
        pulled = jnp.einsum("gij,dgj->dgi", plan_bf16, y_part, preferred_element_type=jnp.float32)
        pushed = jnp.einsum("gij,dgi->dgj", plan_bf16, x_part, preferred_element_type=jnp.float32)
        dx_term = jnp.sum(transport, axis=2)[None] * x_part.astype(jnp.float32) - pulled
        dy_term = jnp.sum(transport, axis=1)[None] * y_part.astype(jnp.float32) - pushed
        dx_total = dx_total + jnp.einsum("gb,dgi->dbi", src_sel, dx_term, precision=highest)
        dy_total = dy_total + jnp.einsum("gb,dgi->dbi", tgt_sel, dy_term, precision=highest)
        return ((dx_total, dy_total), None)

    start_grads = (
        jnp.zeros((feat_width, src_blocks, BLK), jnp.float32),
        jnp.zeros((feat_width, tgt_blocks, BLK), jnp.float32),
    )
    (dx_total, dy_total), _ = lax.scan(
        gradient_group,
        start_grads,
        (src_sel_groups, tgt_sel_groups, kernel.reshape(group_count, group_size, BLK, BLK)),
    )
    tgt_grad = lax.psum(dy_total.reshape(feat_width, tgt_cells), "src")
    hidden_blocks = src_hidden.reshape(feat_width, src_blocks, BLK)
    grad_share = lax.psum_scatter(dx_total, "tgt", scatter_dimension=1, tiled=True)
    share_blocks = grad_share.shape[1]
    first_block = lax.axis_index("tgt") * share_blocks
    hidden_share = lax.dynamic_slice_in_dim(hidden_blocks, first_block, share_blocks, 1)
    batch_share = lax.dynamic_slice_in_dim(block_batch, first_block, share_blocks, 0)
    outer = (
        jnp.einsum("dbi,ebi->bde", hidden_share.astype(jnp.float32), grad_share, precision=highest)
        / BLK
    )
    wanted = jnp.arange(ENC_DEV * lax.axis_size(("src", "tgt")), dtype=jnp.int32)
    owners = (batch_share[None, :] == wanted[:, None]).astype(jnp.float32)
    adapter_grad = lax.psum_scatter(
        jnp.einsum("kb,bde->kde", owners, outer, precision=highest),
        ("src", "tgt"),
        scatter_dimension=0,
        tiled=True,
    )
    return (src_potential, tgt_potential, tgt_grad, adapter_grad)


def solution(mesh):
    in_specs = (
        P(None, "src"),
        P(None, "tgt"),
        P(None, "src"),
        P("src"),
        P("tgt"),
        P("src", "tgt", None),
        P("src", "tgt"),
        P("src"),
    )
    out_specs = (P("src"), P("tgt"), P(None, "tgt"), P(("src", "tgt"), None, None))
    return jax.shard_map(
        per_device, mesh=mesh, in_specs=in_specs, out_specs=out_specs, check_vma=False
    )
```

profile of v0, /device:TPU:0, one launch (start us, length us, event | category | flops | bytes accessed | tf_op | source)
XLA Modules:
  0.0 1027.3 jit_solution(16935787503366914984)
XLA Ops:
  17.6 84.6 %while.23 = (s32[]{:T(128)}, f32[8,64,128,128]{3,2,1,0:T(8,128)}, f32[8,64,128]{2,1,0:T(8,128)S(1)}, f32[128,128]{1,0:T(8,128)S(1)}, f32[8,64,128]{2,1,0:T(8,128...) while((s32[]{:T(128)}, f32[8,64,128,128]{3,2,1,0:T(8,128)}, ...), condition=%wide.region_3.4_spmd, body=%wide.region_2.3_spmd.sunk | while | flops 435159040 | bytes 21334412 | solution.py:64
  102.5 55.7 %fusion.97 = f32[512,1,128]{2,1,0:T(1,128)S(1)} fusion(f32[512,128,128]{2,1,0:T(8,128)} %bitcast.228, f32[512,128,1]{1,2,0:T(1,128)S(1)} %bitcast.246), kind=kOutput, calls=%fused_computation.137 | convolution fusion | flops 100663296 | bytes 34078720 | tf_op jit(solution)/shard_map/pij,pj->pi/dot_general | solution.py:74
  160.0 32.0 %fusion.98 = f32[512,1,128]{2,1,0:T(1,128)S(1)} fusion(f32[512,128,128]{2,1,0:T(8,128)} %bitcast.229, f32[512,128,1]{1,2,0:T(1,128)S(1)} %bitcast.248), kind=kOutput, calls=%fused_computation.138 | convolution fusion | flops 100663296 | bytes 34078720 | tf_op jit(solution)/shard_map/pij,pi->pj/dot_general | solution.py:75
  197.7 32.3 %fusion.100 = f32[512,1,128]{2,1,0:T(1,128)S(1)} fusion(f32[512,128,128]{2,1,0:T(8,128)} %bitcast.230, f32[512,128,1]{1,2,0:T(1,128)S(1)} %bitcast.249), kind=kOutput, calls=%fused_computation.140 | convolution fusion | flops 100663296 | bytes 34078720 | tf_op jit(solution)/shard_map/pij,pi->pj/dot_general | solution.py:75
  231.3 53.3 %all-reduce.12.cloned.1.call-done = (f32[16384]{0:T(1024)}, f32[16384]{0:T(1024)}) async-done(((f32[16384]{0:T(1024)}, f32[16384]{0:T(1024)}), (f32[16384]{0:T(1024)}, f32[16384]{0:T(1024)})) %all-reduce.12.cloned.1.call-update) | async-done | bytes 131088 | tf_op jit(solution)/shard_map/psum | solution.py:79
  285.8 55.9 %fusion.99 = f32[512,1,128]{2,1,0:T(1,128)S(1)} fusion(f32[512,128,128]{2,1,0:T(8,128)} %bitcast.231, f32[512,128,1]{1,2,0:T(1,128)S(1)} %bitcast.247), kind=kOutput, calls=%fused_computation.139 | convolution fusion | flops 100663296 | bytes 34078720 | tf_op jit(solution)/shard_map/pij,pj->pi/dot_general | solution.py:74
  343.7 33.0 %all-reduce.8.cloned.1.call-done = f32[16384]{0:T(1024)} async-done(((f32[16384]{0:T(1024)}), f32[16384]{0:T(1024)}) %all-reduce.8.cloned.1.call-update) | async-done | bytes 65552 | tf_op jit(solution)/shard_map/psum | solution.py:78
  378.3 330.9 %while.24 = (s32[]{:T(128)}, f32[64,128,128]{1,2,0:T(8,128)}, f32[64,128,128]{1,2,0:T(8,128)}, f32[8,64,128]{2,1,0:T(8,128)S(1)}, f32[128,128]{1,0:T(8,128)}, /*...) while((s32[]{:T(128)}, f32[64,128,128]{1,2,0:T(8,128)}, ...), condition=%wide.region_11.12_spmd.clone, body=%wide.region_8.11_spmd.clone.sunk | while | flops 2191507456 | bytes 61508292 | solution.py:110
  432.3 11.2 %bitcast_add_fusion.5 = f32[64,128,128]{1,2,0:T(8,128)} fusion(f32[64,128,128]{1,2,0:T(8,128)} %get-tuple-element.360, f32[64,64,128]{2,1,0:T(8,128)} %fusion.193, bf16[64,64,128]{2,1,0:T(8,128)(2,1)} %fusion.187, pred[]{:T(512)S(6)} %compare.16, f32[64,128]{1,0:T(8,128)S(1)} %get-tuple-element.315, f32[8,64,128]{2,1,0:T(8,128)} %get-tuple-element.376, ...), kind=kOutput, calls=%fused_computation.23.clone.1 | convolution fusion | flops 808976384 | bytes 11600385 | tf_op jit(solution)/shard_map/while/body/eval_jaxpr/gb,dgi->dbi/dot_general | solution.py:103
  448.2 11.3 %bitcast_add_fusion.4 = f32[64,128,128]{1,2,0:T(8,128)} fusion(f32[64,128,128]{1,2,0:T(8,128)} %get-tuple-element.359, f32[64,64,128]{2,1,0:T(8,128)S(1)} %fusion.190, bf16[64,64,128]{2,1,0:T(8,128)(2,1)S(1)} %fusion.191, pred[]{:T(512)S(6)} %compare.16, f32[64,128]{1,0:T(8,128)S(1)} %get-tuple-element.314, ...), kind=kOutput, calls=%fused_computation.24.clone.1 | convolution fusion | flops 808976384 | bytes 11599877 | tf_op jit(solution)/shard_map/while/body/eval_jaxpr/gb,dgi->dbi/dot_general | solution.py:102
  473.9 11.2 %bitcast_add_fusion.5 = f32[64,128,128]{1,2,0:T(8,128)} fusion(f32[64,128,128]{1,2,0:T(8,128)} %get-tuple-element.360, f32[64,64,128]{2,1,0:T(8,128)} %fusion.193, bf16[64,64,128]{2,1,0:T(8,128)(2,1)} %fusion.187, pred[]{:T(512)S(6)} %compare.16, f32[64,128]{1,0:T(8,128)S(1)} %get-tuple-element.315, f32[8,64,128]{2,1,0:T(8,128)} %get-tuple-element.376, ...), kind=kOutput, calls=%fused_computation.23.clone.1 | convolution fusion | flops 808976384 | bytes 11600385 | tf_op jit(solution)/shard_map/while/body/eval_jaxpr/gb,dgi->dbi/dot_general | solution.py:103
  489.8 11.3 %bitcast_add_fusion.4 = f32[64,128,128]{1,2,0:T(8,128)} fusion(f32[64,128,128]{1,2,0:T(8,128)} %get-tuple-element.359, f32[64,64,128]{2,1,0:T(8,128)S(1)} %fusion.190, bf16[64,64,128]{2,1,0:T(8,128)(2,1)S(1)} %fusion.191, pred[]{:T(512)S(6)} %compare.16, f32[64,128]{1,0:T(8,128)S(1)} %get-tuple-element.314, ...), kind=kOutput, calls=%fused_computation.24.clone.1 | convolution fusion | flops 808976384 | bytes 11599877 | tf_op jit(solution)/shard_map/while/body/eval_jaxpr/gb,dgi->dbi/dot_general | solution.py:102
  515.5 11.2 %bitcast_add_fusion.5 = f32[64,128,128]{1,2,0:T(8,128)} fusion(f32[64,128,128]{1,2,0:T(8,128)} %get-tuple-element.360, f32[64,64,128]{2,1,0:T(8,128)} %fusion.193, bf16[64,64,128]{2,1,0:T(8,128)(2,1)} %fusion.187, pred[]{:T(512)S(6)} %compare.16, f32[64,128]{1,0:T(8,128)S(1)} %get-tuple-element.315, f32[8,64,128]{2,1,0:T(8,128)} %get-tuple-element.376, ...), kind=kOutput, calls=%fused_computation.23.clone.1 | convolution fusion | flops 808976384 | bytes 11600385 | tf_op jit(solution)/shard_map/while/body/eval_jaxpr/gb,dgi->dbi/dot_general | solution.py:103
  531.4 11.3 %bitcast_add_fusion.4 = f32[64,128,128]{1,2,0:T(8,128)} fusion(f32[64,128,128]{1,2,0:T(8,128)} %get-tuple-element.359, f32[64,64,128]{2,1,0:T(8,128)S(1)} %fusion.190, bf16[64,64,128]{2,1,0:T(8,128)(2,1)S(1)} %fusion.191, pred[]{:T(512)S(6)} %compare.16, f32[64,128]{1,0:T(8,128)S(1)} %get-tuple-element.314, ...), kind=kOutput, calls=%fused_computation.24.clone.1 | convolution fusion | flops 808976384 | bytes 11599877 | tf_op jit(solution)/shard_map/while/body/eval_jaxpr/gb,dgi->dbi/dot_general | solution.py:102
  557.0 11.2 %bitcast_add_fusion.5 = f32[64,128,128]{1,2,0:T(8,128)} fusion(f32[64,128,128]{1,2,0:T(8,128)} %get-tuple-element.360, f32[64,64,128]{2,1,0:T(8,128)} %fusion.193, bf16[64,64,128]{2,1,0:T(8,128)(2,1)} %fusion.187, pred[]{:T(512)S(6)} %compare.16, f32[64,128]{1,0:T(8,128)S(1)} %get-tuple-element.315, f32[8,64,128]{2,1,0:T(8,128)} %get-tuple-element.376, ...), kind=kOutput, calls=%fused_computation.23.clone.1 | convolution fusion | flops 808976384 | bytes 11600385 | tf_op jit(solution)/shard_map/while/body/eval_jaxpr/gb,dgi->dbi/dot_general | solution.py:103
  572.9 11.3 %bitcast_add_fusion.4 = f32[64,128,128]{1,2,0:T(8,128)} fusion(f32[64,128,128]{1,2,0:T(8,128)} %get-tuple-element.359, f32[64,64,128]{2,1,0:T(8,128)S(1)} %fusion.190, bf16[64,64,128]{2,1,0:T(8,128)(2,1)S(1)} %fusion.191, pred[]{:T(512)S(6)} %compare.16, f32[64,128]{1,0:T(8,128)S(1)} %get-tuple-element.314, ...), kind=kOutput, calls=%fused_computation.24.clone.1 | convolution fusion | flops 808976384 | bytes 11599877 | tf_op jit(solution)/shard_map/while/body/eval_jaxpr/gb,dgi->dbi/dot_general | solution.py:102
  598.6 11.2 %bitcast_add_fusion.5 = f32[64,128,128]{1,2,0:T(8,128)} fusion(f32[64,128,128]{1,2,0:T(8,128)} %get-tuple-element.360, f32[64,64,128]{2,1,0:T(8,128)} %fusion.193, bf16[64,64,128]{2,1,0:T(8,128)(2,1)} %fusion.187, pred[]{:T(512)S(6)} %compare.16, f32[64,128]{1,0:T(8,128)S(1)} %get-tuple-element.315, f32[8,64,128]{2,1,0:T(8,128)} %get-tuple-element.376, ...), kind=kOutput, calls=%fused_computation.23.clone.1 | convolution fusion | flops 808976384 | bytes 11600385 | tf_op jit(solution)/shard_map/while/body/eval_jaxpr/gb,dgi->dbi/dot_general | solution.py:103
  614.5 11.3 %bitcast_add_fusion.4 = f32[64,128,128]{1,2,0:T(8,128)} fusion(f32[64,128,128]{1,2,0:T(8,128)} %get-tuple-element.359, f32[64,64,128]{2,1,0:T(8,128)S(1)} %fusion.190, bf16[64,64,128]{2,1,0:T(8,128)(2,1)S(1)} %fusion.191, pred[]{:T(512)S(6)} %compare.16, f32[64,128]{1,0:T(8,128)S(1)} %get-tuple-element.314, ...), kind=kOutput, calls=%fused_computation.24.clone.1 | convolution fusion | flops 808976384 | bytes 11599877 | tf_op jit(solution)/shard_map/while/body/eval_jaxpr/gb,dgi->dbi/dot_general | solution.py:102
  640.2 11.2 %bitcast_add_fusion.5 = f32[64,128,128]{1,2,0:T(8,128)} fusion(f32[64,128,128]{1,2,0:T(8,128)} %get-tuple-element.360, f32[64,64,128]{2,1,0:T(8,128)} %fusion.193, bf16[64,64,128]{2,1,0:T(8,128)(2,1)} %fusion.187, pred[]{:T(512)S(6)} %compare.16, f32[64,128]{1,0:T(8,128)S(1)} %get-tuple-element.315, f32[8,64,128]{2,1,0:T(8,128)} %get-tuple-element.376, ...), kind=kOutput, calls=%fused_computation.23.clone.1 | convolution fusion | flops 808976384 | bytes 11600385 | tf_op jit(solution)/shard_map/while/body/eval_jaxpr/gb,dgi->dbi/dot_general | solution.py:103
  656.1 11.3 %bitcast_add_fusion.4 = f32[64,128,128]{1,2,0:T(8,128)} fusion(f32[64,128,128]{1,2,0:T(8,128)} %get-tuple-element.359, f32[64,64,128]{2,1,0:T(8,128)S(1)} %fusion.190, bf16[64,64,128]{2,1,0:T(8,128)(2,1)S(1)} %fusion.191, pred[]{:T(512)S(6)} %compare.16, f32[64,128]{1,0:T(8,128)S(1)} %get-tuple-element.314, ...), kind=kOutput, calls=%fused_computation.24.clone.1 | convolution fusion | flops 808976384 | bytes 11599877 | tf_op jit(solution)/shard_map/while/body/eval_jaxpr/gb,dgi->dbi/dot_general | solution.py:102
  697.7 11.3 %bitcast_add_fusion.4 = f32[64,128,128]{1,2,0:T(8,128)} fusion(f32[64,128,128]{1,2,0:T(8,128)} %get-tuple-element.359, f32[64,64,128]{2,1,0:T(8,128)S(1)} %fusion.190, bf16[64,64,128]{2,1,0:T(8,128)(2,1)S(1)} %fusion.191, pred[]{:T(512)S(6)} %compare.16, f32[64,128]{1,0:T(8,128)S(1)} %get-tuple-element.314, ...), kind=kOutput, calls=%fused_computation.24.clone.1 | convolution fusion | flops 808976384 | bytes 11599877 | tf_op jit(solution)/shard_map/while/body/eval_jaxpr/gb,dgi->dbi/dot_general | solution.py:102
  729.5 61.7 %reduce-scatter.3.cloned.1.call-done = f32[64,32,128]{2,0,1:T(8,128)} async-done(((f32[64,128,128]{2,0,1:T(8,128)}), f32[64,32,128]{2,0,1:T(8,128)}) %reduce-scatter.3.cloned.1.call-update) | async-done | bytes 1048592 | tf_op jit(solution)/shard_map/reduce_scatter | solution.py:117
  796.3 79.4 %all-reduce.10.cloned.1.call-done = f32[64,16384]{1,0:T(8,128)} async-done(((f32[64,16384]{1,0:T(8,128)}), f32[64,16384]{1,0:T(8,128)}) %all-reduce.10.cloned.1.call-update) | async-done | bytes 4194320 | tf_op jit(solution)/shard_map/psum | solution.py:115
  875.7 139.8 %reduce-scatter.5.cloned.1.call-done = f32[1,64,64]{2,1,0:T(8,128)} async-done(((f32[32,64,64]{2,1,0:T(8,128)}), f32[1,64,64]{2,1,0:T(8,128)}) %reduce-scatter.5.cloned.1.call-update) | async-done | bytes 16400 | tf_op jit(solution)/shard_map/reduce_scatter | solution.py:128
  (218 shorter events, 321.8 us)
Async XLA Ops:
  7.2 189.4 %all-reduce.6.cloned.1.call-start = ((), (), s32[]{:S(2)}) async-start(), calls=%async_computation.2 | async-start | bytes 131072 | tf_op jit(solution)/shard_map/psum | solution.py:78
  17.6 84.6 %copy-start.9 = (s32[1,1,512]{2,1,0:T(1,128)S(1)}, s32[1,1,512]{2,1,0:T(1,128)}, u32[]{:S(2)}) copy-start(s32[1,1,512]{2,1,0:T(1,128)} %param.17) | copy-start | bytes 6148
  159.4 125.2 %all-reduce.12.cloned.1.call-start = ((), (), s32[]{:S(2)}) async-start(), calls=%async_computation.7 | async-start | bytes 262144 | tf_op jit(solution)/shard_map/psum | solution.py:79
  160.0 36.6 %copy-start.5 = (f32[16384]{0:T(1024)S(1)}, f32[16384]{0:T(1024)}, u32[]{:S(2)}) copy-start(f32[16384]{0:T(1024)} %param.15) | copy-start | bytes 196612
  197.7 86.9 %copy-start.4 = (f32[16384]{0:T(1024)S(1)}, f32[16384]{0:T(1024)}, u32[]{:S(2)}) copy-start(f32[16384]{0:T(1024)} %param.16) | copy-start | bytes 196612
  231.2 145.4 %all-reduce.8.cloned.1.call-start = ((), (), s32[]{:S(2)}) async-start(), calls=%async_computation.3 | async-start | bytes 131072 | tf_op jit(solution)/shard_map/psum | solution.py:78
  285.8 57.1 %copy-start.7 = (f32[16384]{0:T(1024)S(1)}, f32[16384]{0:T(1024)}, u32[]{:S(2)}) copy-start(f32[16384]{0:T(1024)} %get-tuple-element.184) | copy-start | bytes 196612
  285.8 57.1 %copy-start.8 = (f32[16384]{0:T(1024)S(1)}, f32[16384]{0:T(1024)}, u32[]{:S(2)}) copy-start(f32[16384]{0:T(1024)} %get-tuple-element.185) | copy-start | bytes 196612
  285.8 90.9 %copy-start.6 = (f32[16384]{0:T(1024)S(1)}, f32[16384]{0:T(1024)}, u32[]{:S(2)}) copy-start(f32[16384]{0:T(1024)} %all-reduce.6.cloned.1.call-done) | copy-start | bytes 196612
  342.8 448.4 %reduce-scatter.3.cloned.1.call-start = ((), (), s32[]{:S(2)}) async-start(), calls=%async_computation.5 | async-start | bytes 5242880 | tf_op jit(solution)/shard_map/reduce_scatter | solution.py:117
  381.0 9.7 copy-start.1
  392.9 10.6 %copy-start.2 = (bf16[64,64,128]{2,1,0:T(8,128)(2,1)S(1)}, bf16[64,64,128]{2,1,0:T(8,128)(2,1)}, u32[]{:S(2)}) copy-start(bf16[64,64,128]{2,1,0:T(8,128)(2,1)} %fusion.187) | copy-start | bytes 3145732 | tf_op jit(solution)/shard_map/while
  420.4 9.7 copy-start.1
  432.3 11.2 %copy-start.2 = (bf16[64,64,128]{2,1,0:T(8,128)(2,1)S(1)}, bf16[64,64,128]{2,1,0:T(8,128)(2,1)}, u32[]{:S(2)}) copy-start(bf16[64,64,128]{2,1,0:T(8,128)(2,1)} %fusion.187) | copy-start | bytes 3145732 | tf_op jit(solution)/shard_map/while
  462.0 9.7 copy-start.1
  473.9 11.2 %copy-start.2 = (bf16[64,64,128]{2,1,0:T(8,128)(2,1)S(1)}, bf16[64,64,128]{2,1,0:T(8,128)(2,1)}, u32[]{:S(2)}) copy-start(bf16[64,64,128]{2,1,0:T(8,128)(2,1)} %fusion.187) | copy-start | bytes 3145732 | tf_op jit(solution)/shard_map/while
  503.6 9.7 copy-start.1
  515.5 11.2 %copy-start.2 = (bf16[64,64,128]{2,1,0:T(8,128)(2,1)S(1)}, bf16[64,64,128]{2,1,0:T(8,128)(2,1)}, u32[]{:S(2)}) copy-start(bf16[64,64,128]{2,1,0:T(8,128)(2,1)} %fusion.187) | copy-start | bytes 3145732 | tf_op jit(solution)/shard_map/while
  557.0 11.2 %copy-start.2 = (bf16[64,64,128]{2,1,0:T(8,128)(2,1)S(1)}, bf16[64,64,128]{2,1,0:T(8,128)(2,1)}, u32[]{:S(2)}) copy-start(bf16[64,64,128]{2,1,0:T(8,128)(2,1)} %fusion.187) | copy-start | bytes 3145732 | tf_op jit(solution)/shard_map/while
  598.6 11.2 %copy-start.2 = (bf16[64,64,128]{2,1,0:T(8,128)(2,1)S(1)}, bf16[64,64,128]{2,1,0:T(8,128)(2,1)}, u32[]{:S(2)}) copy-start(bf16[64,64,128]{2,1,0:T(8,128)(2,1)} %fusion.187) | copy-start | bytes 3145732 | tf_op jit(solution)/shard_map/while
  640.2 11.2 %copy-start.2 = (bf16[64,64,128]{2,1,0:T(8,128)(2,1)S(1)}, bf16[64,64,128]{2,1,0:T(8,128)(2,1)}, u32[]{:S(2)}) copy-start(bf16[64,64,128]{2,1,0:T(8,128)(2,1)} %fusion.187) | copy-start | bytes 3145732 | tf_op jit(solution)/shard_map/while
  681.7 11.2 %copy-start.2 = (bf16[64,64,128]{2,1,0:T(8,128)(2,1)S(1)}, bf16[64,64,128]{2,1,0:T(8,128)(2,1)}, u32[]{:S(2)}) copy-start(bf16[64,64,128]{2,1,0:T(8,128)(2,1)} %fusion.187) | copy-start | bytes 3145732 | tf_op jit(solution)/shard_map/while
  714.6 161.1 %all-reduce.10.cloned.1.call-start = ((), (), s32[]{:S(2)}) async-start(), calls=%async_computation.4 | async-start | bytes 8388608 | tf_op jit(solution)/shard_map/psum | solution.py:115
  727.2 288.3 %reduce-scatter.5.cloned.1.call-start = ((), (), s32[]{:S(2)}) async-start(), calls=%async_computation.6 | async-start | bytes 1081344 | tf_op jit(solution)/shard_map/reduce_scatter | solution.py:128
  (14 other events, 58.3 us)
Sparse Core Ops, SparseCore 0:
  159.5 36.9 all-reduce.5
  231.4 53.2 all-reduce.11
  343.0 33.6 all-reduce.7
  714.7 76.4 reduce-scatter.2
  794.3 81.3 all-reduce.9
  878.4 137.0 reduce-scatter.4
where the time goes:
time: 1040 us; the launch traced here: 1030 us
  matrix products  558 us (54%)
  waiting for transfers between devices  371 us (36%)
  other arithmetic  41.4 us (4%)
  local copies, waits for them, and re-layouts  40.3 us (4%)
  between operations  15.4 us (1%)
    reduce_scatter x1, waiting for transfers between devices, per_device(): lax.psum_scatter(jnp.einsum('kb,bde->kde', owners, outer, precision=highe...  140 us
    dot_general x2, matrix products, per_device(): row_slots = jnp.einsum('pij,pj->pi', kernel, tgt_picked, precision=highest)  112 us
    dot_general x8, matrix products, gradient_group(): jnp.einsum('gb,dgi->dbi', tgt_sel, dy_term, precision=highest)  89 us
    dot_general x8, matrix products, gradient_group(): jnp.einsum('gb,dgi->dbi', src_sel, dx_term, precision=highest)  88.5 us
    psum x1, waiting for transfers between devices, per_device(): tgt_grad = lax.psum(dy_total.reshape(feat_width, tgt_cells), 'src')  79.4 us
    dot_general x2, matrix products, per_device(): col_slots = jnp.einsum('pij,pi->pj', kernel, src_picked, precision=highest)  64.3 us
    reduce_scatter x1, waiting for transfers between devices, per_device(): lax.psum_scatter(dx_total, 'tgt', scatter_dimension=1, tiled=True)  61.7 us
    psum x1, waiting for transfers between devices, per_device(): col_sums = lax.psum(col_part, 'src')  53.3 us
  transfers between devices with their start and end apart: 6, of which 6 were waited for; matrix products, arithmetic and copies ran while one was open for 5% of the time, Pallas kernels for 0%

commit v1 on v0

--- a/solution.py
+++ b/solution.py
@@ -76,7 +76,15 @@
         row_part = jnp.dot(src_select.T, row_slots, precision=highest).reshape(src_cells)
         col_part = jnp.dot(tgt_select.T, col_slots, precision=highest).reshape(tgt_cells)
         row_sums = lax.psum(row_part, "tgt")
-        col_sums = lax.psum(col_part, "src")
+        n_shards = lax.axis_size("src")
+        col_sums, mixed_arr = (col_part, 0)
+        while 1 << mixed_arr < n_shards:
+            sides = []
+            for k0 in tuple(range(n_shards)):
+                sides.append((k0, k0 ^ 1 << mixed_arr))
+            arr_out = lax.ppermute(col_sums, "src", sides)
+            col_sums = col_sums + arr_out
+            mixed_arr = mixed_arr + 1
         src_scale, tgt_scale = (
             rescale(src_scale, src_mass, row_sums),
             rescale(tgt_scale, tgt_mass, col_sums),

time: 1040 us -> 999 us (0.961)
  waiting for transfers between devices: 371 us -> 325 us
    psum x1 -> x0, waiting for transfers between devices: 53.3 us -> none  [per_device(): col_sums = lax.psum(col_part, 'src')]
    psum x2 -> x1, waiting for transfers between devices: 36.4 us -> 35.1 us  [per_device(): row_sums = lax.psum(row_part, 'tgt')]
  transfers between devices with their start and end apart: 6 -> 10, of which waited for: 6 -> 9; matrix products, arithmetic and copies ran while one was open for 5% -> 8% of each run, Pallas kernels for 0% -> 0%
where the time goes in v1:
time: 999 us; the launch traced here: 986 us
  matrix products  556 us (56%)
  waiting for transfers between devices  325 us (33%)
  other arithmetic  40.6 us (4%)
  local copies, waits for them, and re-layouts  40.4 us (4%)
  between operations  15.1 us (2%)
    reduce_scatter x1, waiting for transfers between devices, per_device(): lax.psum_scatter(jnp.einsum('kb,bde->kde', owners, outer, precision=highe...  140 us
    dot_general x2, matrix products, per_device(): row_slots = jnp.einsum('pij,pj->pi', kernel, tgt_picked, precision=highest)  112 us
    dot_general x8, matrix products, gradient_group(): jnp.einsum('gb,dgi->dbi', tgt_sel, dy_term, precision=highest)  89.1 us
    dot_general x8, matrix products, gradient_group(): jnp.einsum('gb,dgi->dbi', src_sel, dx_term, precision=highest)  88.5 us
    psum x1, waiting for transfers between devices, per_device(): tgt_grad = lax.psum(dy_total.reshape(feat_width, tgt_cells), 'src')  79.5 us
    dot_general x2, matrix products, per_device(): col_slots = jnp.einsum('pij,pi->pj', kernel, src_picked, precision=highest)  64 us
    reduce_scatter x1, waiting for transfers between devices, per_device(): lax.psum_scatter(dx_total, 'tgt', scatter_dimension=1, tiled=True)  61.7 us
    dot_general x8, matrix products, kernel_group(): jnp.einsum('dgi,dgj->gij', x_part, y_part, preferred_element_type=jnp.flo...  53 us
  transfers between devices with their start and end apart: 10, of which 9 were waited for; matrix products, arithmetic and copies ran while one was open for 8% of the time, Pallas kernels for 0%

profile of v1, /device:TPU:0, one launch (start us, length us, event | category | flops | bytes accessed | tf_op | source)
XLA Modules:
  0.0 986.2 jit_solution(5025419893124097393)
XLA Ops:
  17.6 84.6 %while.23 = (s32[]{:T(128)}, f32[8,64,128,128]{3,2,1,0:T(8,128)}, f32[8,64,128]{2,1,0:T(8,128)S(1)}, f32[128,128]{1,0:T(8,128)S(1)}, f32[8,64,128]{2,1,0:T(8,128...) while((s32[]{:T(128)}, f32[8,64,128,128]{3,2,1,0:T(8,128)}, ...), condition=%wide.region_3.4_spmd, body=%wide.region_2.3_spmd.sunk | while | flops 435159040 | bytes 21334412 | solution.py:64
  102.5 31.9 %fusion.97 = f32[512,1,128]{2,1,0:T(1,128)S(1)} fusion(f32[512,128,128]{2,1,0:T(8,128)} %bitcast.228, f32[512,128,1]{1,2,0:T(1,128)S(1)} %bitcast.248), kind=kOutput, calls=%fused_computation.137 | convolution fusion | flops 100663296 | bytes 34078720 | tf_op jit(solution)/shard_map/pij,pi->pj/dot_general | solution.py:75
  139.3 55.9 %fusion.96 = f32[512,1,128]{2,1,0:T(1,128)S(1)} fusion(f32[512,128,128]{2,1,0:T(8,128)} %bitcast.229, f32[512,128,1]{1,2,0:T(1,128)S(1)} %bitcast.247), kind=kOutput, calls=%fused_computation.136 | convolution fusion | flops 100663296 | bytes 34078720 | tf_op jit(solution)/shard_map/pij,pj->pi/dot_general | solution.py:74
  199.9 56.1 %fusion.98 = f32[512,1,128]{2,1,0:T(1,128)S(1)} fusion(f32[512,128,128]{2,1,0:T(8,128)} %bitcast.230, f32[512,128,1]{1,2,0:T(1,128)S(1)} %bitcast.246), kind=kOutput, calls=%fused_computation.138 | convolution fusion | flops 100663296 | bytes 34078720 | tf_op jit(solution)/shard_map/pij,pj->pi/dot_general | solution.py:74
  257.2 35.1 %all-reduce.6.cloned.1.call-done = (f32[16384]{0:T(1024)}, f32[16384]{0:T(1024)}) async-done(((f32[16384]{0:T(1024)}, f32[16384]{0:T(1024)}), (f32[16384]{0:T(1024)}, f32[16384]{0:T(1024)})) %all-reduce.6.cloned.1.call-update) | async-done | bytes 131088 | tf_op jit(solution)/shard_map/psum | solution.py:78
  293.6 32.1 %fusion.99 = f32[512,1,128]{2,1,0:T(1,128)S(1)} fusion(f32[512,128,128]{2,1,0:T(8,128)} %bitcast.231, f32[512,128,1]{1,2,0:T(1,128)S(1)} %bitcast.249), kind=kOutput, calls=%fused_computation.139 | convolution fusion | flops 100663296 | bytes 34078720 | tf_op jit(solution)/shard_map/pij,pi->pj/dot_general | solution.py:75
  337.0 331.1 %while.24 = (s32[]{:T(128)}, f32[64,128,128]{1,2,0:T(8,128)}, f32[64,128,128]{1,2,0:T(8,128)}, f32[8,64,128]{2,1,0:T(8,128)S(1)}, f32[128,128]{1,0:T(8,128)}, /*...) while((s32[]{:T(128)}, f32[64,128,128]{1,2,0:T(8,128)}, ...), condition=%wide.region_9.10_spmd.clone, body=%wide.region_6.9_spmd.clone.sunk | while | flops 2191507456 | bytes 61508292 | solution.py:118
  391.0 11.2 %bitcast_add_fusion.5 = f32[64,128,128]{1,2,0:T(8,128)} fusion(f32[64,128,128]{1,2,0:T(8,128)} %get-tuple-element.360, f32[64,64,128]{2,1,0:T(8,128)} %fusion.192, bf16[64,64,128]{2,1,0:T(8,128)(2,1)} %fusion.186, pred[]{:T(512)S(6)} %compare.16, f32[64,128]{1,0:T(8,128)S(1)} %get-tuple-element.315, f32[8,64,128]{2,1,0:T(8,128)} %get-tuple-element.376, ...), kind=kOutput, calls=%fused_computation.23.clone.1 | convolution fusion | flops 808976384 | bytes 11600385 | tf_op jit(solution)/shard_map/while/body/eval_jaxpr/gb,dgi->dbi/dot_general | solution.py:111
  407.0 11.3 %bitcast_add_fusion.4 = f32[64,128,128]{1,2,0:T(8,128)} fusion(f32[64,128,128]{1,2,0:T(8,128)} %get-tuple-element.359, f32[64,64,128]{2,1,0:T(8,128)S(1)} %fusion.189, bf16[64,64,128]{2,1,0:T(8,128)(2,1)S(1)} %fusion.190, pred[]{:T(512)S(6)} %compare.16, f32[64,128]{1,0:T(8,128)S(1)} %get-tuple-element.314, ...), kind=kOutput, calls=%fused_computation.24.clone.1 | convolution fusion | flops 808976384 | bytes 11599877 | tf_op jit(solution)/shard_map/while/body/eval_jaxpr/gb,dgi->dbi/dot_general | solution.py:110
  432.6 11.2 %bitcast_add_fusion.5 = f32[64,128,128]{1,2,0:T(8,128)} fusion(f32[64,128,128]{1,2,0:T(8,128)} %get-tuple-element.360, f32[64,64,128]{2,1,0:T(8,128)} %fusion.192, bf16[64,64,128]{2,1,0:T(8,128)(2,1)} %fusion.186, pred[]{:T(512)S(6)} %compare.16, f32[64,128]{1,0:T(8,128)S(1)} %get-tuple-element.315, f32[8,64,128]{2,1,0:T(8,128)} %get-tuple-element.376, ...), kind=kOutput, calls=%fused_computation.23.clone.1 | convolution fusion | flops 808976384 | bytes 11600385 | tf_op jit(solution)/shard_map/while/body/eval_jaxpr/gb,dgi->dbi/dot_general | solution.py:111
  448.6 11.3 %bitcast_add_fusion.4 = f32[64,128,128]{1,2,0:T(8,128)} fusion(f32[64,128,128]{1,2,0:T(8,128)} %get-tuple-element.359, f32[64,64,128]{2,1,0:T(8,128)S(1)} %fusion.189, bf16[64,64,128]{2,1,0:T(8,128)(2,1)S(1)} %fusion.190, pred[]{:T(512)S(6)} %compare.16, f32[64,128]{1,0:T(8,128)S(1)} %get-tuple-element.314, ...), kind=kOutput, calls=%fused_computation.24.clone.1 | convolution fusion | flops 808976384 | bytes 11599877 | tf_op jit(solution)/shard_map/while/body/eval_jaxpr/gb,dgi->dbi/dot_general | solution.py:110
  474.2 11.2 %bitcast_add_fusion.5 = f32[64,128,128]{1,2,0:T(8,128)} fusion(f32[64,128,128]{1,2,0:T(8,128)} %get-tuple-element.360, f32[64,64,128]{2,1,0:T(8,128)} %fusion.192, bf16[64,64,128]{2,1,0:T(8,128)(2,1)} %fusion.186, pred[]{:T(512)S(6)} %compare.16, f32[64,128]{1,0:T(8,128)S(1)} %get-tuple-element.315, f32[8,64,128]{2,1,0:T(8,128)} %get-tuple-element.376, ...), kind=kOutput, calls=%fused_computation.23.clone.1 | convolution fusion | flops 808976384 | bytes 11600385 | tf_op jit(solution)/shard_map/while/body/eval_jaxpr/gb,dgi->dbi/dot_general | solution.py:111
  490.2 11.3 %bitcast_add_fusion.4 = f32[64,128,128]{1,2,0:T(8,128)} fusion(f32[64,128,128]{1,2,0:T(8,128)} %get-tuple-element.359, f32[64,64,128]{2,1,0:T(8,128)S(1)} %fusion.189, bf16[64,64,128]{2,1,0:T(8,128)(2,1)S(1)} %fusion.190, pred[]{:T(512)S(6)} %compare.16, f32[64,128]{1,0:T(8,128)S(1)} %get-tuple-element.314, ...), kind=kOutput, calls=%fused_computation.24.clone.1 | convolution fusion | flops 808976384 | bytes 11599877 | tf_op jit(solution)/shard_map/while/body/eval_jaxpr/gb,dgi->dbi/dot_general | solution.py:110
  515.8 11.2 %bitcast_add_fusion.5 = f32[64,128,128]{1,2,0:T(8,128)} fusion(f32[64,128,128]{1,2,0:T(8,128)} %get-tuple-element.360, f32[64,64,128]{2,1,0:T(8,128)} %fusion.192, bf16[64,64,128]{2,1,0:T(8,128)(2,1)} %fusion.186, pred[]{:T(512)S(6)} %compare.16, f32[64,128]{1,0:T(8,128)S(1)} %get-tuple-element.315, f32[8,64,128]{2,1,0:T(8,128)} %get-tuple-element.376, ...), kind=kOutput, calls=%fused_computation.23.clone.1 | convolution fusion | flops 808976384 | bytes 11600385 | tf_op jit(solution)/shard_map/while/body/eval_jaxpr/gb,dgi->dbi/dot_general | solution.py:111
  531.7 11.3 %bitcast_add_fusion.4 = f32[64,128,128]{1,2,0:T(8,128)} fusion(f32[64,128,128]{1,2,0:T(8,128)} %get-tuple-element.359, f32[64,64,128]{2,1,0:T(8,128)S(1)} %fusion.189, bf16[64,64,128]{2,1,0:T(8,128)(2,1)S(1)} %fusion.190, pred[]{:T(512)S(6)} %compare.16, f32[64,128]{1,0:T(8,128)S(1)} %get-tuple-element.314, ...), kind=kOutput, calls=%fused_computation.24.clone.1 | convolution fusion | flops 808976384 | bytes 11599877 | tf_op jit(solution)/shard_map/while/body/eval_jaxpr/gb,dgi->dbi/dot_general | solution.py:110
  557.4 11.2 %bitcast_add_fusion.5 = f32[64,128,128]{1,2,0:T(8,128)} fusion(f32[64,128,128]{1,2,0:T(8,128)} %get-tuple-element.360, f32[64,64,128]{2,1,0:T(8,128)} %fusion.192, bf16[64,64,128]{2,1,0:T(8,128)(2,1)} %fusion.186, pred[]{:T(512)S(6)} %compare.16, f32[64,128]{1,0:T(8,128)S(1)} %get-tuple-element.315, f32[8,64,128]{2,1,0:T(8,128)} %get-tuple-element.376, ...), kind=kOutput, calls=%fused_computation.23.clone.1 | convolution fusion | flops 808976384 | bytes 11600385 | tf_op jit(solution)/shard_map/while/body/eval_jaxpr/gb,dgi->dbi/dot_general | solution.py:111
  573.3 11.3 %bitcast_add_fusion.4 = f32[64,128,128]{1,2,0:T(8,128)} fusion(f32[64,128,128]{1,2,0:T(8,128)} %get-tuple-element.359, f32[64,64,128]{2,1,0:T(8,128)S(1)} %fusion.189, bf16[64,64,128]{2,1,0:T(8,128)(2,1)S(1)} %fusion.190, pred[]{:T(512)S(6)} %compare.16, f32[64,128]{1,0:T(8,128)S(1)} %get-tuple-element.314, ...), kind=kOutput, calls=%fused_computation.24.clone.1 | convolution fusion | flops 808976384 | bytes 11599877 | tf_op jit(solution)/shard_map/while/body/eval_jaxpr/gb,dgi->dbi/dot_general | solution.py:110
  599.0 11.2 %bitcast_add_fusion.5 = f32[64,128,128]{1,2,0:T(8,128)} fusion(f32[64,128,128]{1,2,0:T(8,128)} %get-tuple-element.360, f32[64,64,128]{2,1,0:T(8,128)} %fusion.192, bf16[64,64,128]{2,1,0:T(8,128)(2,1)} %fusion.186, pred[]{:T(512)S(6)} %compare.16, f32[64,128]{1,0:T(8,128)S(1)} %get-tuple-element.315, f32[8,64,128]{2,1,0:T(8,128)} %get-tuple-element.376, ...), kind=kOutput, calls=%fused_computation.23.clone.1 | convolution fusion | flops 808976384 | bytes 11600385 | tf_op jit(solution)/shard_map/while/body/eval_jaxpr/gb,dgi->dbi/dot_general | solution.py:111
  614.9 11.3 %bitcast_add_fusion.4 = f32[64,128,128]{1,2,0:T(8,128)} fusion(f32[64,128,128]{1,2,0:T(8,128)} %get-tuple-element.359, f32[64,64,128]{2,1,0:T(8,128)S(1)} %fusion.189, bf16[64,64,128]{2,1,0:T(8,128)(2,1)S(1)} %fusion.190, pred[]{:T(512)S(6)} %compare.16, f32[64,128]{1,0:T(8,128)S(1)} %get-tuple-element.314, ...), kind=kOutput, calls=%fused_computation.24.clone.1 | convolution fusion | flops 808976384 | bytes 11599877 | tf_op jit(solution)/shard_map/while/body/eval_jaxpr/gb,dgi->dbi/dot_general | solution.py:110
  640.6 11.2 %bitcast_add_fusion.5 = f32[64,128,128]{1,2,0:T(8,128)} fusion(f32[64,128,128]{1,2,0:T(8,128)} %get-tuple-element.360, f32[64,64,128]{2,1,0:T(8,128)} %fusion.192, bf16[64,64,128]{2,1,0:T(8,128)(2,1)} %fusion.186, pred[]{:T(512)S(6)} %compare.16, f32[64,128]{1,0:T(8,128)S(1)} %get-tuple-element.315, f32[8,64,128]{2,1,0:T(8,128)} %get-tuple-element.376, ...), kind=kOutput, calls=%fused_computation.23.clone.1 | convolution fusion | flops 808976384 | bytes 11600385 | tf_op jit(solution)/shard_map/while/body/eval_jaxpr/gb,dgi->dbi/dot_general | solution.py:111
  656.5 11.3 %bitcast_add_fusion.4 = f32[64,128,128]{1,2,0:T(8,128)} fusion(f32[64,128,128]{1,2,0:T(8,128)} %get-tuple-element.359, f32[64,64,128]{2,1,0:T(8,128)S(1)} %fusion.189, bf16[64,64,128]{2,1,0:T(8,128)(2,1)S(1)} %fusion.190, pred[]{:T(512)S(6)} %compare.16, f32[64,128]{1,0:T(8,128)S(1)} %get-tuple-element.314, ...), kind=kOutput, calls=%fused_computation.24.clone.1 | convolution fusion | flops 808976384 | bytes 11599877 | tf_op jit(solution)/shard_map/while/body/eval_jaxpr/gb,dgi->dbi/dot_general | solution.py:110
  688.4 61.7 %reduce-scatter.3.cloned.1.call-done = f32[64,32,128]{2,0,1:T(8,128)} async-done(((f32[64,128,128]{2,0,1:T(8,128)}), f32[64,32,128]{2,0,1:T(8,128)}) %reduce-scatter.3.cloned.1.call-update) | async-done | bytes 1048592 | tf_op jit(solution)/shard_map/reduce_scatter | solution.py:125
  755.3 79.5 %all-reduce.4.cloned.1.call-done = f32[64,16384]{1,0:T(8,128)} async-done(((f32[64,16384]{1,0:T(8,128)}), f32[64,16384]{1,0:T(8,128)}) %all-reduce.4.cloned.1.call-update) | async-done | bytes 4194320 | tf_op jit(solution)/shard_map/psum | solution.py:123
  834.8 139.9 %reduce-scatter.5.cloned.1.call-done = f32[1,64,64]{2,1,0:T(8,128)} async-done(((f32[32,64,64]{2,1,0:T(8,128)}), f32[1,64,64]{2,1,0:T(8,128)}) %reduce-scatter.5.cloned.1.call-update) | async-done | bytes 16400 | tf_op jit(solution)/shard_map/reduce_scatter | solution.py:136
  (226 shorter events, 320.4 us)
Async XLA Ops:
  7.2 285.2 %all-reduce.6.cloned.1.call-start = ((), (), s32[]{:S(2)}) async-start(), calls=%async_computation.5 | async-start | bytes 262144 | tf_op jit(solution)/shard_map/psum | solution.py:78
  17.6 84.6 %copy-start.8 = (s32[1,1,512]{2,1,0:T(1,128)S(1)}, s32[1,1,512]{2,1,0:T(1,128)}, u32[]{:S(2)}) copy-start(s32[1,1,512]{2,1,0:T(1,128)} %param.17) | copy-start | bytes 6148
  135.0 1.5 collective-permute-start
  136.4 58.8 %collective-permute-start.1 = (f32[16384]{0:T(1024)S(1)}, f32[16384]{0:T(1024)S(1)}, u32[]{:S(2)}, u32[]{:S(2)}) collective-permute-start(f32[16384]{0:T(1024)S(1)} %add.79), channel_id=1, source_target_pairs={{0,8},{4,12},{8,0},{12,4},{16,24},{20,28},{24,16},{28,20},{1,9},{5... | collective-permute-start | bytes 196616 | tf_op jit(solution)/shard_map/ppermute | solution.py:85
  139.3 60.2 %copy-start.4 = (f32[16384]{0:T(1024)S(1)}, f32[16384]{0:T(1024)}, u32[]{:S(2)}) copy-start(f32[16384]{0:T(1024)} %param.16) | copy-start | bytes 196612
  195.2 4.3 collective-permute-start.2
  199.9 92.5 %copy-start.5 = (f32[16384]{0:T(1024)S(1)}, f32[16384]{0:T(1024)}, u32[]{:S(2)}) copy-start(f32[16384]{0:T(1024)} %param.15) | copy-start | bytes 196612
  257.2 493.0 %reduce-scatter.3.cloned.1.call-start = ((), (), s32[]{:S(2)}) async-start(), calls=%async_computation.3 | async-start | bytes 5242880 | tf_op jit(solution)/shard_map/reduce_scatter | solution.py:125
  293.5 39.9 %copy-start.6 = (f32[16384]{0:T(1024)S(1)}, f32[16384]{0:T(1024)}, u32[]{:S(2)}) copy-start(f32[16384]{0:T(1024)} %get-tuple-element.185) | copy-start | bytes 196612
  293.5 39.8 %copy-start.7 = (f32[16384]{0:T(1024)S(1)}, f32[16384]{0:T(1024)}, u32[]{:S(2)}) copy-start(f32[16384]{0:T(1024)} %get-tuple-element.184) | copy-start | bytes 196612
  326.2 1.3 collective-permute-start.3
  327.5 4.3 collective-permute-start.4
  331.9 4.3 collective-permute-start.5
  339.7 9.7 copy-start.1
  351.6 10.6 %copy-start.2 = (bf16[64,64,128]{2,1,0:T(8,128)(2,1)S(1)}, bf16[64,64,128]{2,1,0:T(8,128)(2,1)}, u32[]{:S(2)}) copy-start(bf16[64,64,128]{2,1,0:T(8,128)(2,1)} %fusion.186) | copy-start | bytes 3145732 | tf_op jit(solution)/shard_map/while
  391.0 11.2 %copy-start.2 = (bf16[64,64,128]{2,1,0:T(8,128)(2,1)S(1)}, bf16[64,64,128]{2,1,0:T(8,128)(2,1)}, u32[]{:S(2)}) copy-start(bf16[64,64,128]{2,1,0:T(8,128)(2,1)} %fusion.186) | copy-start | bytes 3145732 | tf_op jit(solution)/shard_map/while
  432.6 11.2 %copy-start.2 = (bf16[64,64,128]{2,1,0:T(8,128)(2,1)S(1)}, bf16[64,64,128]{2,1,0:T(8,128)(2,1)}, u32[]{:S(2)}) copy-start(bf16[64,64,128]{2,1,0:T(8,128)(2,1)} %fusion.186) | copy-start | bytes 3145732 | tf_op jit(solution)/shard_map/while
  474.2 11.2 %copy-start.2 = (bf16[64,64,128]{2,1,0:T(8,128)(2,1)S(1)}, bf16[64,64,128]{2,1,0:T(8,128)(2,1)}, u32[]{:S(2)}) copy-start(bf16[64,64,128]{2,1,0:T(8,128)(2,1)} %fusion.186) | copy-start | bytes 3145732 | tf_op jit(solution)/shard_map/while
  515.8 11.2 %copy-start.2 = (bf16[64,64,128]{2,1,0:T(8,128)(2,1)S(1)}, bf16[64,64,128]{2,1,0:T(8,128)(2,1)}, u32[]{:S(2)}) copy-start(bf16[64,64,128]{2,1,0:T(8,128)(2,1)} %fusion.186) | copy-start | bytes 3145732 | tf_op jit(solution)/shard_map/while
  557.4 11.2 %copy-start.2 = (bf16[64,64,128]{2,1,0:T(8,128)(2,1)S(1)}, bf16[64,64,128]{2,1,0:T(8,128)(2,1)}, u32[]{:S(2)}) copy-start(bf16[64,64,128]{2,1,0:T(8,128)(2,1)} %fusion.186) | copy-start | bytes 3145732 | tf_op jit(solution)/shard_map/while
  599.0 11.2 %copy-start.2 = (bf16[64,64,128]{2,1,0:T(8,128)(2,1)S(1)}, bf16[64,64,128]{2,1,0:T(8,128)(2,1)}, u32[]{:S(2)}) copy-start(bf16[64,64,128]{2,1,0:T(8,128)(2,1)} %fusion.186) | copy-start | bytes 3145732 | tf_op jit(solution)/shard_map/while
  640.6 11.2 %copy-start.2 = (bf16[64,64,128]{2,1,0:T(8,128)(2,1)S(1)}, bf16[64,64,128]{2,1,0:T(8,128)(2,1)}, u32[]{:S(2)}) copy-start(bf16[64,64,128]{2,1,0:T(8,128)(2,1)} %fusion.186) | copy-start | bytes 3145732 | tf_op jit(solution)/shard_map/while
  673.5 161.3 %all-reduce.4.cloned.1.call-start = ((), (), s32[]{:S(2)}) async-start(), calls=%async_computation.2 | async-start | bytes 8388608 | tf_op jit(solution)/shard_map/psum | solution.py:123
  686.1 288.7 %reduce-scatter.5.cloned.1.call-start = ((), (), s32[]{:S(2)}) async-start(), calls=%async_computation.4 | async-start | bytes 1081344 | tf_op jit(solution)/shard_map/reduce_scatter | solution.py:136
  (17 other events, 87.5 us)
Sparse Core Ops, SparseCore 0:
  257.3 35.0 all-reduce.5
  673.6 76.5 reduce-scatter.2
  753.4 81.3 all-reduce.3
  837.5 137.2 reduce-scatter.4
